TPU v7x, 32 devices: a whole 2x2x4 slice. The times are simulated.
32 devices in a mesh: dp: 8 (over y, x, core), seq: 4 (over z).
Axes of the slice: x: 2, y: 2, z: 4, core: 2. Of those that a mesh axis runs over, the one named last changes fastest.
Arguments:
- tokens_in: bfloat16 [16, 580, 1024], P('dp', 'seq'), may hold values from -6 to 6
- cotangent: bfloat16 [16, 580, 1024], P('dp', 'seq'), may hold values from -6 to 6
- group_count: int32 [8], P('dp'), may hold values from 1 to 2, as said below
- key_mask: int32 [16, 580], P('dp'), may hold values from 0 to 1, as said below
- ln1_gain: float32 [1024], P(('dp', 'seq')), may hold values from 0.5 to 1.5
- ln1_shift: float32 [1024], P(('dp', 'seq')), may hold values from -3 to 3
- w_query: float32 [1024, 1024], P(('dp', 'seq')), may hold values from -0.25 to 0.25
- b_query: float32 [1024], P(('dp', 'seq')), may hold values from -3 to 3
- w_key: float32 [1024, 1024], P(('dp', 'seq')), may hold values from -0.1875 to 0.1875
- w_value: float32 [1024, 1024], P(('dp', 'seq')), may hold values from -0.1875 to 0.1875
- b_value: float32 [1024], P(('dp', 'seq')), may hold values from -0.6 to 0.6
- w_out: float32 [1024, 1024], P(('dp', 'seq')), may hold values from -1.5 to 1.5
- b_out: float32 [1024], P(('dp', 'seq')), may hold values from -3 to 3
- ln2_gain: float32 [1024], P(('dp', 'seq')), may hold values from 0.5 to 1.5
- ln2_shift: float32 [1024], P(('dp', 'seq')), may hold values from -3 to 3
- w_up: float32 [1024, 4096], P(('dp', 'seq')), may hold values from -0.1875 to 0.1875
- b_up: float32 [4096], P(('dp', 'seq')), may hold values from -3 to 3
- w_down: float32 [4096, 1024], P(('dp', 'seq')), may hold values from -0.09375 to 0.09375
- b_down: float32 [1024], P(('dp', 'seq')), may hold values from -3 to 3
Outputs:
- block_out: bfloat16 [16, 580, 1024], P('dp', 'seq')
- input_grad: bfloat16 [16, 580, 1024], P('dp', 'seq')
- grad_ln1_gain: float32 [1024], P(('dp', 'seq'))
- grad_ln1_shift: float32 [1024], P(('dp', 'seq'))
- grad_w_query: float32 [1024, 1024], P(('dp', 'seq'))
- grad_b_query: float32 [1024], P(('dp', 'seq'))
- grad_w_key: float32 [1024, 1024], P(('dp', 'seq'))
- grad_w_value: float32 [1024, 1024], P(('dp', 'seq'))
- grad_b_value: float32 [1024], P(('dp', 'seq'))
- grad_w_out: float32 [1024, 1024], P(('dp', 'seq'))
- grad_b_out: float32 [1024], P(('dp', 'seq'))
- grad_ln2_gain: float32 [1024], P(('dp', 'seq'))
- grad_ln2_shift: float32 [1024], P(('dp', 'seq'))
- grad_w_up: float32 [1024, 4096], P(('dp', 'seq'))
- grad_b_up: float32 [4096], P(('dp', 'seq'))
- grad_w_down: float32 [4096, 1024], P(('dp', 'seq'))
- grad_b_down: float32 [1024], P(('dp', 'seq'))
Inputs may be any that keep to these rules, and one draw needn't show every extreme that they name: A data group's images fill its first group_count slots; some group holds 2. `key_mask`: the first token of every image is a key; positions 577 and later never are.
All inputs are finite; a program needn't handle non-finite values.
Results may differ from a plain program's by a relative error of at most 0.013.
The roundings to bfloat16 on the way count: a program that leaves them out, or rounds other values in their place, can miss the bound.
Values may be sent and summed in bfloat16 or wider, within the bound.
No kernel may reach another device: no remote copies, remote signals or barrier semaphores. Data moves between devices by JAX's collectives and lax.ppermute only.
A program may use at most 192 MiB of HBM per device.

v0:
```python
import jax
import jax.numpy as jnp
from jax import lax
from jax.sharding import PartitionSpec as P

HD = 64
EPSILON = 1e-05
SLOPE = 1.702
MASKED = -1000000000.0


def norm_stats(values):
    center = values - jnp.mean(values, axis=-1, keepdims=True)
    inverse = lax.rsqrt(jnp.mean(center * center, axis=-1, keepdims=True) + EPSILON)
    return (center * inverse, inverse)


def norm_back(incoming, normal, inverse, gain):
    scaled = incoming * gain
    rows_grad = inverse * (
        scaled
        - jnp.mean(scaled, axis=-1, keepdims=True)
        - normal * jnp.mean(scaled * normal, axis=-1, keepdims=True)
    )
    return (rows_grad, jnp.sum(incoming * normal, axis=0), jnp.sum(incoming, axis=0))


def product(left, right):
    return jnp.dot(left, right, preferred_element_type=jnp.float32)


def contract_rows(left, right):
    return lax.dot_general(
        left, right, (((0,), (0,)), ((), ())), preferred_element_type=jnp.float32
    )


def contract_cols(left, right):
    return lax.dot_general(
        left, right, (((1,), (1,)), ((), ())), preferred_element_type=jnp.float32
    )


def split_heads(stacked):
    length = stacked.shape[0]
    heads_here = stacked.shape[2] // HD
    queries = stacked[:, 0].reshape(length, heads_here, HD)
    keys_all = stacked[:, 1].reshape(length, heads_here, HD)
    values_all = stacked[:, 2].reshape(length, heads_here, HD)
    return (queries, keys_all, values_all)


def masked_scores(queries, keys_all, key_keep):
    scores = jnp.einsum(
        "qhd,khd->hqk", queries, keys_all, preferred_element_type=jnp.float32
    ) * HD ** (-0.5)
    return jnp.where(key_keep[None, None, :] > 0, scores, MASKED)


def attend_image(paired):
    stacked, key_keep = paired
    queries, keys_all, values_all = split_heads(stacked)
    scores = masked_scores(queries, keys_all, key_keep)
    row_peak = jnp.max(scores, axis=-1, keepdims=True)
    weights_exp = jnp.exp(scores - row_peak)
    row_total = jnp.sum(weights_exp, axis=-1, keepdims=True)
    weights_soft = weights_exp / row_total
    mixed_out = jnp.einsum(
        "hqk,khd->qhd",
        weights_soft.astype(jnp.bfloat16),
        values_all,
        preferred_element_type=jnp.float32,
    )
    log_total = (row_peak + jnp.log(row_total))[..., 0]
    return (mixed_out.reshape(stacked.shape[0], stacked.shape[2]).astype(jnp.bfloat16), log_total)


def attend_back(packed):
    stacked, grad_mixed, log_total, key_keep = packed
    queries, keys_all, values_all = split_heads(stacked)
    scores = masked_scores(queries, keys_all, key_keep)
    weights_soft = jnp.exp(scores - log_total[..., None])
    grad_mix = grad_mixed.reshape(queries.shape)
    grad_values = jnp.einsum(
        "hqk,qhd->khd",
        weights_soft.astype(jnp.bfloat16),
        grad_mix,
        preferred_element_type=jnp.float32,
    )
    grad_weights = jnp.einsum(
        "qhd,khd->hqk", grad_mix, values_all, preferred_element_type=jnp.float32
    )
    row_inner = jnp.sum(grad_weights * weights_soft, axis=-1, keepdims=True)
    grad_scores = (weights_soft * (grad_weights - row_inner)).astype(jnp.bfloat16)
    grad_queries = jnp.einsum(
        "hqk,khd->qhd", grad_scores, keys_all, preferred_element_type=jnp.float32
    ) * HD ** (-0.5)
    grad_keys = jnp.einsum(
        "hqk,qhd->khd", grad_scores, queries, preferred_element_type=jnp.float32
    ) * HD ** (-0.5)
    length = stacked.shape[0]
    return jnp.stack(
        [
            grad_queries.reshape(length, -1),
            grad_keys.reshape(length, -1),
            grad_values.reshape(length, -1),
        ],
        axis=1,
    ).astype(jnp.bfloat16)


def per_device(
    tokens_in,
    cotangent,
    group_count,
    key_mask,
    ln1_gain,
    ln1_shift,
    w_query,
    b_query,
    w_key,
    w_value,
    b_value,
    w_out,
    b_out,
    ln2_gain,
    ln2_shift,
    w_up,
    b_up,
    w_down,
    b_down,
):
    slot_count, tok_dev, width = tokens_in.shape
    row_count = slot_count * tok_dev
    shared = (
        lax.all_gather(ln1_gain.astype(jnp.bfloat16), ("dp", "seq"), axis=0, tiled=True),
        lax.all_gather(ln1_shift.astype(jnp.bfloat16), ("dp", "seq"), axis=0, tiled=True),
        lax.all_gather(w_query.astype(jnp.bfloat16), ("dp", "seq"), axis=0, tiled=True),
        lax.all_gather(b_query.astype(jnp.bfloat16), ("dp", "seq"), axis=0, tiled=True),
        lax.all_gather(w_key.astype(jnp.bfloat16), ("dp", "seq"), axis=0, tiled=True),
        lax.all_gather(w_value.astype(jnp.bfloat16), ("dp", "seq"), axis=0, tiled=True),
        lax.all_gather(b_value.astype(jnp.bfloat16), ("dp", "seq"), axis=0, tiled=True),
        lax.all_gather(w_out.astype(jnp.bfloat16), ("dp", "seq"), axis=0, tiled=True),
        lax.all_gather(b_out.astype(jnp.bfloat16), ("dp", "seq"), axis=0, tiled=True),
        lax.all_gather(ln2_gain.astype(jnp.bfloat16), ("dp", "seq"), axis=0, tiled=True),
        lax.all_gather(ln2_shift.astype(jnp.bfloat16), ("dp", "seq"), axis=0, tiled=True),
        lax.all_gather(w_up.astype(jnp.bfloat16), ("dp", "seq"), axis=0, tiled=True),
        lax.all_gather(b_up.astype(jnp.bfloat16), ("dp", "seq"), axis=0, tiled=True),
        lax.all_gather(w_down.astype(jnp.bfloat16), ("dp", "seq"), axis=0, tiled=True),
        lax.all_gather(b_down.astype(jnp.bfloat16), ("dp", "seq"), axis=0, tiled=True),
    )
    (
        gain_one,
        shift_one,
        query_w,
        query_b,
        key_w,
        value_w,
        value_b,
        out_w,
        out_b,
        gain_two,
        shift_two,
        up_w,
        up_b,
        down_w,
        down_b,
    ) = shared
    live_slot = (jnp.arange(slot_count) < group_count[0]).astype(jnp.float32)[:, None, None]
    inputs = tokens_in.astype(jnp.float32).reshape(row_count, width)
    normal_one, inverse_one = norm_stats(inputs)
    normed_one = (normal_one * gain_one + shift_one).astype(jnp.bfloat16)
    queries = (product(normed_one, query_w) + query_b).astype(jnp.bfloat16)
    keys_all = product(normed_one, key_w).astype(jnp.bfloat16)
    values_all = (product(normed_one, value_w) + value_b).astype(jnp.bfloat16)
    stacked = jnp.stack([queries, keys_all, values_all], axis=1).reshape(
        slot_count, tok_dev, 3, width
    )
    by_heads = lax.all_to_all(stacked, "seq", split_axis=3, concat_axis=1, tiled=True)
    mixed_heads, log_total = lax.map(attend_image, (by_heads, key_mask))
    mixed_tok = lax.all_to_all(mixed_heads, "seq", split_axis=1, concat_axis=2, tiled=True).reshape(
        row_count, width
    )
    middle = inputs + product(mixed_tok, out_w) + out_b
    normal_two, inverse_two = norm_stats(middle)
    normed_two = (normal_two * gain_two + shift_two).astype(jnp.bfloat16)
    hidden = product(normed_two, up_w) + up_b
    gate_sig = jax.nn.sigmoid(SLOPE * hidden)
    activated = (hidden * gate_sig).astype(jnp.bfloat16)
    result = middle + product(activated, down_w) + down_b
    block_out = (result.reshape(slot_count, tok_dev, width) * live_slot).astype(jnp.bfloat16)
    upstream = (cotangent.astype(jnp.float32) * live_slot).reshape(row_count, width)
    upstream_low = upstream.astype(jnp.bfloat16)
    grad_down = contract_rows(activated, upstream_low)
    grad_down_b = jnp.sum(upstream, axis=0)
    grad_act = contract_cols(upstream_low, down_w)
    grad_hidden = (grad_act * (gate_sig + SLOPE * hidden * gate_sig * (1.0 - gate_sig))).astype(
        jnp.bfloat16
    )
    grad_up = contract_rows(normed_two, grad_hidden)
    grad_up_b = jnp.sum(grad_hidden.astype(jnp.float32), axis=0)
    grad_normed_two = contract_cols(grad_hidden, up_w)
    grad_mid, grad_gain_two, grad_shift_two = norm_back(
        grad_normed_two, normal_two, inverse_two, gain_two
    )
    grad_middle = upstream + grad_mid
    branch_low = grad_middle.astype(jnp.bfloat16)
    grad_out = contract_rows(mixed_tok, branch_low)
    grad_out_b = jnp.sum(branch_low.astype(jnp.float32), axis=0)
    grad_mixed = (
        contract_cols(branch_low, out_w).astype(jnp.bfloat16).reshape(slot_count, tok_dev, width)
    )
    grad_by_heads = lax.all_to_all(grad_mixed, "seq", split_axis=2, concat_axis=1, tiled=True)
    grad_stacked = lax.map(attend_back, (by_heads, grad_by_heads, log_total, key_mask))
    grad_tok = lax.all_to_all(grad_stacked, "seq", split_axis=1, concat_axis=3, tiled=True).reshape(
        row_count, 3, width
    )
    grad_q_rows = grad_tok[:, 0]
    grad_k_rows = grad_tok[:, 1]
    grad_v_rows = grad_tok[:, 2]
    grad_query = contract_rows(normed_one, grad_q_rows)
    grad_query_b = jnp.sum(grad_q_rows.astype(jnp.float32), axis=0)
    grad_key = contract_rows(normed_one, grad_k_rows)
    grad_value = contract_rows(normed_one, grad_v_rows)
    grad_value_b = jnp.sum(grad_v_rows.astype(jnp.float32), axis=0)
    grad_normed_one = (
        contract_cols(grad_q_rows, query_w)
        + contract_cols(grad_k_rows, key_w)
        + contract_cols(grad_v_rows, value_w)
    )
    grad_first, grad_gain_one, grad_shift_one = norm_back(
        grad_normed_one, normal_one, inverse_one, gain_one
    )
    input_grad = (grad_middle + grad_first).astype(jnp.bfloat16).reshape(slot_count, tok_dev, width)
    every_shard = (
        lax.psum_scatter(grad_gain_one, ("dp", "seq"), scatter_dimension=0, tiled=True),
        lax.psum_scatter(grad_shift_one, ("dp", "seq"), scatter_dimension=0, tiled=True),
        lax.psum_scatter(grad_query, ("dp", "seq"), scatter_dimension=0, tiled=True),
        lax.psum_scatter(grad_query_b, ("dp", "seq"), scatter_dimension=0, tiled=True),
        lax.psum_scatter(grad_key, ("dp", "seq"), scatter_dimension=0, tiled=True),
        lax.psum_scatter(grad_value, ("dp", "seq"), scatter_dimension=0, tiled=True),
        lax.psum_scatter(grad_value_b, ("dp", "seq"), scatter_dimension=0, tiled=True),
        lax.psum_scatter(grad_out, ("dp", "seq"), scatter_dimension=0, tiled=True),
        lax.psum_scatter(grad_out_b, ("dp", "seq"), scatter_dimension=0, tiled=True),
        lax.psum_scatter(grad_gain_two, ("dp", "seq"), scatter_dimension=0, tiled=True),
        lax.psum_scatter(grad_shift_two, ("dp", "seq"), scatter_dimension=0, tiled=True),
        lax.psum_scatter(grad_up, ("dp", "seq"), scatter_dimension=0, tiled=True),
        lax.psum_scatter(grad_up_b, ("dp", "seq"), scatter_dimension=0, tiled=True),
        lax.psum_scatter(grad_down, ("dp", "seq"), scatter_dimension=0, tiled=True),
        lax.psum_scatter(grad_down_b, ("dp", "seq"), scatter_dimension=0, tiled=True),
    )
    return (block_out, input_grad) + tuple(every_shard)


def solution(mesh):
    return jax.shard_map(
        per_device,
        mesh=mesh,
        in_specs=(
            P("dp", "seq", None),
            P("dp", "seq", None),
            P("dp"),
            P("dp", None),
            P(("dp", "seq")),
            P(("dp", "seq")),
            P(("dp", "seq"), None),
            P(("dp", "seq")),
            P(("dp", "seq"), None),
            P(("dp", "seq"), None),
            P(("dp", "seq")),
            P(("dp", "seq"), None),
            P(("dp", "seq")),
            P(("dp", "seq")),
            P(("dp", "seq")),
            P(("dp", "seq"), None),
            P(("dp", "seq")),
            P(("dp", "seq"), None),
            P(("dp", "seq")),
        ),
        out_specs=(
            P("dp", "seq", None),
            P("dp", "seq", None),
            P(("dp", "seq")),
            P(("dp", "seq")),
            P(("dp", "seq"), None),
            P(("dp", "seq")),
            P(("dp", "seq"), None),
            P(("dp", "seq"), None),
            P(("dp", "seq")),
            P(("dp", "seq"), None),
            P(("dp", "seq")),
            P(("dp", "seq")),
            P(("dp", "seq")),
            P(("dp", "seq"), None),
            P(("dp", "seq")),
            P(("dp", "seq"), None),
            P(("dp", "seq")),
        ),
        check_vma=False,
    )
```

profile of v0, /device:TPU:0, one launch (start us, length us, event | category | flops | bytes accessed | tf_op | source)
XLA Modules:
  0.0 1859.5 jit_solution(8726085616884812577)
XLA Ops:
  7.3 1.7 convert_element_type.187
  9.1 1.5 convert_element_type.185
  10.8 1.5 convert_element_type.181
  12.4 1.5 convert_element_type.191
  14.0 1.8 convert_element_type.199
  18.8 42.5 %all-reduce.18 = (bf16[1024]{0:T(1024)(128)(2,1)S(1)}, bf16[1024]{0:T(1024)(128)(2,1)S(1)}, bf16[1024]{0:T(1024)(128)(2,1)S(1)}, bf16[1024]{0:T(1024)(128)(2,1)S...) all-reduce(bf16[1024]{0:T(1024)(128)(2,1)S(1)} %dynamic-update-slic, ...), channel_id=1, replica_groups=mesh['dp'=8,'seq'=4] {'dp','seq'}, use_global_device_ids=true, to_apply=%add.1 | all-reduce | flops 8192 | bytes 32768
  63.5 7.6 all-gather.12.cloned.1.call-done
  71.1 3.2 fusion.21
  75.5 54.4 %all-gather.10.cloned.1.call-done = bf16[1024,1024]{1,0:T(8,128)(2,1)} async-done(((bf16[32,1024]{1,0:T(8,128)(2,1)}), bf16[1024,1024]{1,0:T(8,128)(2,1)}) %all-gather.10.cloned.1.call-update) | async-done | bytes 2097168 | tf_op jit(solution)/shard_map/all_gather | solution.py:140
  129.9 2.4 convolution_convert_fusion.1
  132.5 56.2 %all-gather.8.cloned.1.call-done = bf16[1024,1024]{1,0:T(8,128)(2,1)} async-done(((bf16[32,1024]{1,0:T(8,128)(2,1)}), bf16[1024,1024]{1,0:T(8,128)(2,1)}) %all-gather.8.cloned.1.call-update) | async-done | bytes 2097168 | tf_op jit(solution)/shard_map/all_gather | solution.py:138
  188.7 2.6 fusion.20
  193.5 5.7 copy.101
  199.3 3.9 all-to-all-start
  203.1 80.6 %all-to-all-done = bf16[2,145,3,1024]{1,0,2,3:T(2,128)(2,1)S(1)} async-done(((bf16[2,145,3,1024]{1,0,2,3:T(2,128)(2,1)}), bf16[2,145,3,1024]{1,0,2,3:T(2,128)(2,1)S(1)}, u32[]{:S(2)}, u32[]{:S(2)}) %all-to-all-start) | async-done | bytes 1781792 | tf_op jit(solution)/shard_map/all_to_all | solution.py:179
  283.8 4.1 copy.145
  287.8 5.4 reshape.335
  293.2 9.8 while.22
  293.5 1.4 fusion.98
  296.3 1.7 fusion.100
  298.4 1.4 fusion.98
  301.2 1.7 fusion.100
  304.2 3.5 all-to-all-start.1
  308.4 82.6 %all-gather = bf16[32,1,128]{2,1,0:T(2,128)(2,1)S(1)} all-gather(bf16[1,1,128]{2,1,0:T(2,128)(2,1)S(1)} %convert_bitcast_fusion), channel_id=1, replica_groups=mesh['dp'=8,'seq'=4] {'dp','seq'}, dimensions={0}, use_global_device_ids=true | all-gather | bytes 8448 | tf_op jit(solution)/shard_map/all_gather | solution.py:148
  392.6 3.0 fusion.36
  396.0 8.8 convolution_add_fusion
  404.8 42.8 %all-gather.18.cloned.1.call-done = bf16[4096,1024]{1,0:T(8,128)(2,1)} async-done(((bf16[128,1024]{1,0:T(8,128)(2,1)}), bf16[4096,1024]{1,0:T(8,128)(2,1)}) %all-gather.18.cloned.1.call-update) | async-done | bytes 8388624 | tf_op jit(solution)/shard_map/all_gather | solution.py:149
  447.7 8.7 fusion.19
  456.4 2.5 reshape.310
  458.8 3.7 fusion.32
  462.6 2.4 reshape.311
  465.0 9.0 convert_reduce_fusion
  474.0 6.4 multiply_reduce_fusion.1
  484.3 3.7 copy.109
  487.9 4.3 all-to-all-start.2
  492.3 4.4 fusion.29
  496.7 35.9 %all-to-all-done.2 = bf16[2,145,1024]{1,0,2:T(2,128)(2,1)} async-done(((bf16[2,145,1024]{1,0,2:T(2,128)(2,1)}), bf16[2,145,1024]{1,0,2:T(2,128)(2,1)}, u32[]{:S(2)}, u32[]{:S(2)}) %all-to-all-start.2) | async-done | bytes 593952 | tf_op jit(solution)/shard_map/all_to_all | solution.py:213
  532.6 3.0 copy.147
  535.6 2.7 reshape.334
  538.3 21.9 %while.23 = (s32[]{:T(128)}, bf16[2,580,3,256]{1,3,2,0:T(8,128)(2,1)}, bf16[2,580,3,256]{1,3,2,0:T(8,128)(2,1)S(1)}, s32[2,580]{1,0:T(2,128)S(1)}, f32[2,4,580]{...) while((s32[]{:T(128)}, bf16[2,580,3,256]{1,3,2,0:T(8,128)(2,1)}, ...), condition=%wide.region_12.13_spmd, body=%wide.region_10.12_spmd.sunk | while | flops 884781312 | bytes 63784960 | solution.py:214
  539.7 1.5 fusion.113
  541.2 2.0 multiply_reduce_fusion.10
  543.2 1.9 multiply_convert_fusion.6
  550.6 1.5 fusion.113
  552.1 2.0 multiply_reduce_fusion.10
  554.2 1.9 multiply_convert_fusion.6
  560.1 5.2 copy.114
  565.4 4.5 all-to-all-start.3
  571.3 61.0 %all-to-all-done.3 = bf16[2,580,3,256]{3,0,2,1:T(2,128)(2,1)} async-done(((bf16[2,580,3,256]{3,0,2,1:T(2,128)(2,1)}), bf16[2,580,3,256]{3,0,2,1:T(2,128)(2,1)}, u32[]{:S(2)}, u32[]{:S(2)}) %all-to-all-start.3) | async-done | bytes 1781792 | tf_op jit(solution)/shard_map/all_to_all | solution.py:215
  632.3 1.8 copy.146
  634.1 2.0 copy.116
  636.0 3.0 reshape.313
  639.0 3.3 fusion.23
  642.4 3.3 fusion.22
  645.7 3.4 fusion.25
  650.4 10.0 fusion.33
  661.8 11.0 fusion.26
  675.3 2.6 fusion.24
  683.5 39.7 %all-reduce.17 = (f32[1024]{0:T(1024)S(1)}, f32[1024]{0:T(1024)S(1)}, f32[1024]{0:T(1024)S(1)}, f32[1024]{0:T(1024)S(1)}, f32[1024]{0:T(1024)S(1)}, /*index=5*/f...) all-reduce(f32[1024]{0:T(1024)S(1)} %get-tuple-element.183, ...), channel_id=2, replica_groups=mesh['dp'=8,'seq'=4] {'dp','seq'}, use_global_device_ids=true, to_apply=%region_16.17.clone | all-reduce | flops 12288 | bytes 98304
  728.5 95.1 %reduce-scatter.7.cloned.1.call-done = f32[32,1024]{1,0:T(8,128)} async-done(((f32[1024,1024]{1,0:T(8,128)}), f32[32,1024]{1,0:T(8,128)}) %reduce-scatter.7.cloned.1.call-update) | async-done | bytes 131088 | tf_op jit(solution)/shard_map/reduce_scatter | solution.py:238
  823.6 151.1 %reduce-scatter.9.cloned.1.call-done = f32[32,1024]{1,0:T(8,128)} async-done(((f32[1024,1024]{1,0:T(8,128)}), f32[32,1024]{1,0:T(8,128)}) %reduce-scatter.9.cloned.1.call-update) | async-done | bytes 131088 | tf_op jit(solution)/shard_map/reduce_scatter | solution.py:240
  974.7 150.8 %reduce-scatter.11.cloned.1.call-done = f32[32,1024]{1,0:T(8,128)} async-done(((f32[1024,1024]{1,0:T(8,128)}), f32[32,1024]{1,0:T(8,128)}) %reduce-scatter.11.cloned.1.call-update) | async-done | bytes 131088 | tf_op jit(solution)/shard_map/reduce_scatter | solution.py:241
  1125.5 362.2 %reduce-scatter.15.cloned.1.call-done = f32[32,4096]{1,0:T(8,128)} async-done(((f32[1024,4096]{1,0:T(8,128)}), f32[32,4096]{1,0:T(8,128)}) %reduce-scatter.15.cloned.1.call-update) | async-done | bytes 524304 | tf_op jit(solution)/shard_map/reduce_scatter | solution.py:247
  1487.7 364.7 %reduce-scatter.17.cloned.1.call-done = f32[128,1024]{1,0:T(8,128)} async-done(((f32[4096,1024]{1,0:T(8,128)}), f32[128,1024]{1,0:T(8,128)}) %reduce-scatter.17.cloned.1.call-update) | async-done | bytes 524304 | tf_op jit(solution)/shard_map/reduce_scatter | solution.py:249
  (237 shorter events, 47.1 us)
Async XLA Ops:
  7.2 8.7 copy-start.22
  7.2 9.4 copy-start.35
  7.2 9.4 copy-start.36
  7.2 9.5 copy-start.37
  7.2 9.5 copy-start.38
  7.2 9.5 copy-start.39
  7.3 9.5 copy-start.40
  7.3 9.5 copy-start.41
  7.3 9.5 copy-start.42
  7.3 9.5 copy-start.7
  7.3 63.8 %all-gather.12.cloned.1.call-start = ((), (), s32[]{:S(2)}) async-start(), calls=%async_computation.12 | async-start | bytes 2162688 | tf_op jit(solution)/shard_map/all_gather | solution.py:141
  9.1 120.8 %all-gather.10.cloned.1.call-start = ((), (), s32[]{:S(2)}) async-start(), calls=%async_computation.11 | async-start | bytes 2162688 | tf_op jit(solution)/shard_map/all_gather | solution.py:140
  10.7 178.0 %all-gather.8.cloned.1.call-start = ((), (), s32[]{:S(2)}) async-start(), calls=%async_computation.10 | async-start | bytes 2162688 | tf_op jit(solution)/shard_map/all_gather | solution.py:138
  12.3 380.3 %all-gather.14.cloned.1.call-start = ((), (), s32[]{:S(2)}) async-start(), calls=%async_computation.13 | async-start | bytes 2162688 | tf_op jit(solution)/shard_map/all_gather | solution.py:143
  13.9 382.0 %all-gather.16.cloned.1.call-start = ((), (), s32[]{:S(2)}) async-start(), calls=%async_computation.14 | async-start | bytes 8650752 | tf_op jit(solution)/shard_map/all_gather | solution.py:147
  15.8 431.9 %all-gather.18.cloned.1.call-start = ((), (), s32[]{:S(2)}) async-start(), calls=%async_computation.15 | async-start | bytes 8650752 | tf_op jit(solution)/shard_map/all_gather | solution.py:149
  17.1 57.2 %copy-start.2 = (f32[290,1024]{1,0:T(8,128)}, f32[290,1024]{1,0:T(8,128)S(1)}, u32[]{:S(2)}) copy-start(f32[290,1024]{1,0:T(8,128)S(1)} %reshape.308) | copy-start | bytes 3563524
  61.3 9.8 copy-start.26
  61.3 9.8 copy-start.24
  61.9 9.2 copy-start.16
  62.9 11.4 copy-start.18
  63.1 11.2 copy-start.28
  63.2 11.1 copy-start.30
  63.5 66.4 %copy-start.21 = (bf16[290,1024]{1,0:T(8,128)(2,1)}, bf16[290,1024]{1,0:T(8,128)(2,1)S(1)}, u32[]{:S(2)}) copy-start(bf16[290,1024]{1,0:T(8,128)(2,1)S(1)} %add_convert_fusion.2) | copy-start | bytes 1781764
  199.3 84.5 %all-to-all-start = ((bf16[2,145,3,1024]{1,0,2,3:T(2,128)(2,1)}), bf16[2,145,3,1024]{1,0,2,3:T(2,128)(2,1)S(1)}, u32[]{:S(2)}, u32[]{:S(2)}) async-start(bf16[2,145,3,1024]{1,0,2,3:T(2,128)(2,1)} %copy.101), calls=%async_computation | async-start | bytes 6291456 | tf_op jit(solution)/shard_map/all_to_all | solution.py:179
  287.8 5.4 copy-start.20
  287.8 5.4 copy-start.23
  303.0 5.4 copy-start.43
  304.2 86.8 %all-to-all-start.1 = ((bf16[2,580,256]{2,0,1:T(2,128)(2,1)}), bf16[2,580,256]{2,0,1:T(2,128)(2,1)S(1)}, u32[]{:S(2)}, u32[]{:S(2)}) async-start(bf16[2,580,256]{2,0,1:T(2,128)(2,1)} %copy.105), calls=%async_computation.1 | async-start | bytes 1187840 | tf_op jit(solution)/shard_map/all_to_all | solution.py:181
  395.7 84.8 %copy-start = (f32[290,1024]{1,0:T(8,128)}, f32[290,1024]{1,0:T(8,128)S(1)}, u32[]{:S(2)}) copy-start(f32[290,1024]{1,0:T(8,128)S(1)} %get-tuple-element.246) | copy-start | bytes 3563524
  474.0 6.5 copy-start.12
  474.0 6.5 copy-start.9
  480.5 2.0 copy-start.34
  480.9 1.0 copy-start.4
  484.3 8.0 copy-start.5
  487.9 44.6 %all-to-all-start.2 = ((bf16[2,145,1024]{1,0,2:T(2,128)(2,1)}), bf16[2,145,1024]{1,0,2:T(2,128)(2,1)}, u32[]{:S(2)}, u32[]{:S(2)}) async-start(bf16[2,145,1024]{1,0,2:T(2,128)(2,1)} %copy.109), calls=%async_computation.2 | async-start | bytes 2097152 | tf_op jit(solution)/shard_map/all_to_all | solution.py:213
  492.2 236.2 %reduce-scatter.13.cloned.1.call-start = ((), (), s32[]{:S(2)}) async-start(), calls=%async_computation.19 | async-start | bytes 4325376 | tf_op jit(solution)/shard_map/reduce_scatter | solution.py:243
  546.2 1.6 copy-start.14
  547.9 1.3 copy-start.15
  557.1 1.6 copy-start.14
  558.8 1.3 copy-start.15
  565.3 4.6 copy-start.8
  565.3 4.6 copy-start.17
  565.3 4.6 copy-start.19
  565.3 4.6 copy-start.25
  565.3 4.6 copy-start.27
  565.4 66.9 %all-to-all-start.3 = ((bf16[2,580,3,256]{3,0,2,1:T(2,128)(2,1)}), bf16[2,580,3,256]{3,0,2,1:T(2,128)(2,1)}, u32[]{:S(2)}, u32[]{:S(2)}) async-start(bf16[2,580,3,256]{3,0,2,1:T(2,128)(2,1)} %copy.114), calls=%async_computation.3 | async-start | bytes 3563520 | tf_op jit(solution)/shard_map/all_to_all | solution.py:215
  569.9 253.7 %reduce-scatter.7.cloned.1.call-start = ((), (), s32[]{:S(2)}) async-start(), calls=%async_computation.16 | async-start | bytes 4325376 | tf_op jit(solution)/shard_map/reduce_scatter | solution.py:238
  642.4 332.4 %reduce-scatter.9.cloned.1.call-start = ((), (), s32[]{:S(2)}) async-start(), calls=%async_computation.17 | async-start | bytes 4325376 | tf_op jit(solution)/shard_map/reduce_scatter | solution.py:240
  645.7 479.8 %reduce-scatter.11.cloned.1.call-start = ((), (), s32[]{:S(2)}) async-start(), calls=%async_computation.18 | async-start | bytes 4325376 | tf_op jit(solution)/shard_map/reduce_scatter | solution.py:241
  649.1 1.3 copy-start.1
  649.2 838.6 %reduce-scatter.15.cloned.1.call-start = ((), (), s32[]{:S(2)}) async-start(), calls=%async_computation.20 | async-start | bytes 17301504 | tf_op jit(solution)/shard_map/reduce_scatter | solution.py:247
  660.5 1.3 copy-start.10
  660.5 1191.9 %reduce-scatter.17.cloned.1.call-start = ((), (), s32[]{:S(2)}) async-start(), calls=%async_computation.21 | async-start | bytes 17301504 | tf_op jit(solution)/shard_map/reduce_scatter | solution.py:249
  672.8 1.1 copy-start.11
  675.3 2.6 copy-start.13
  677.9 1.3 copy-start.3
  677.9 1.3 copy-start.29
  677.9 1.3 copy-start.31
  677.9 2.0 copy-start.33
  679.9 1.3 copy-start.6
  681.7 1.8 copy-start.32
Sparse Core Ops, SparseCore 0:
  11.6 59.4 all-gather.11
  74.6 55.2 all-gather.9
  133.4 55.1 all-gather.7
  192.0 93.6 all-gather.13
  289.1 79.6 all-gather.15
  372.1 75.5 all-gather.17
  496.8 176.0 reduce-scatter.12
  675.7 147.7 reduce-scatter.6
  826.4 148.2 reduce-scatter.8
  977.4 148.0 reduce-scatter.10
  1128.4 359.2 reduce-scatter.14
  1490.5 361.9 reduce-scatter.16
where the time goes:
time: 1870 us; the launch traced here: 1860 us
  waiting for transfers between devices  1460 us (78%)
  blocking collectives  165 us (9%)
  matrix products  104 us (6%)
  local copies, waits for them, and re-layouts  69.7 us (4%)
  other arithmetic  25.2 us (1%)
    reduce_scatter x1, waiting for transfers between devices, per_device(): lax.psum_scatter(grad_down, ('dp', 'seq'), scatter_dimension=0, tiled=True)  365 us
    reduce_scatter x1, waiting for transfers between devices, per_device(): lax.psum_scatter(grad_up, ('dp', 'seq'), scatter_dimension=0, tiled=True)  362 us
    reduce_scatter x1, waiting for transfers between devices, per_device(): lax.psum_scatter(grad_key, ('dp', 'seq'), scatter_dimension=0, tiled=True)  151 us
    reduce_scatter x1, waiting for transfers between devices, per_device(): lax.psum_scatter(grad_value, ('dp', 'seq'), scatter_dimension=0, tiled=True)  151 us
    reduce_scatter x1, waiting for transfers between devices, per_device(): lax.psum_scatter(grad_query, ('dp', 'seq'), scatter_dimension=0, tiled=True)  95.1 us
    all_gather x1, blocking collectives, per_device(): lax.all_gather(b_up.astype(jnp.bfloat16), ('dp', 'seq'), axis=0, tiled=True)  82.6 us
    unnamed x2, blocking collectives  82.2 us
    all_to_all x1, waiting for transfers between devices, per_device(): lax.all_to_all(stacked, 'seq', split_axis=3, concat_axis=1, tiled=True)  80.6 us
  transfers between devices with their start and end apart: 16, of which 12 were waited for; matrix products, arithmetic and copies ran while one was open for 8% of the time, Pallas kernels for 0%

commit v1 on v0

--- a/solution.py
+++ b/solution.py
@@ -212,9 +212,12 @@
     )
     grad_by_heads = lax.all_to_all(grad_mixed, "seq", split_axis=2, concat_axis=1, tiled=True)
     grad_stacked = lax.map(attend_back, (by_heads, grad_by_heads, log_total, key_mask))
-    grad_tok = lax.all_to_all(grad_stacked, "seq", split_axis=1, concat_axis=3, tiled=True).reshape(
-        row_count, 3, width
-    )
+    grad_tok = jnp.concatenate(
+        lax.all_to_all(
+            jnp.stack(jnp.split(grad_stacked, lax.axis_size("seq"), axis=1)), "seq", 0, 0
+        ),
+        axis=3,
+    ).reshape(row_count, 3, width)
     grad_q_rows = grad_tok[:, 0]
     grad_k_rows = grad_tok[:, 1]
     grad_v_rows = grad_tok[:, 2]

time: 1870 us -> 1870 us (level)
  no operation moved by 1% of the time
where the time goes in v1:
time: 1870 us; the launch traced here: 1860 us
  waiting for transfers between devices  1460 us (78%)
  blocking collectives  164 us (9%)
  matrix products  104 us (6%)
  local copies, waits for them, and re-layouts  69.3 us (4%)
  other arithmetic  29.4 us (2%)
    reduce_scatter x1, waiting for transfers between devices, per_device(): lax.psum_scatter(grad_down, ('dp', 'seq'), scatter_dimension=0, tiled=True)  365 us
    reduce_scatter x1, waiting for transfers between devices, per_device(): lax.psum_scatter(grad_up, ('dp', 'seq'), scatter_dimension=0, tiled=True)  362 us
    reduce_scatter x1, waiting for transfers between devices, per_device(): lax.psum_scatter(grad_value, ('dp', 'seq'), scatter_dimension=0, tiled=True)  151 us
    reduce_scatter x1, waiting for transfers between devices, per_device(): lax.psum_scatter(grad_key, ('dp', 'seq'), scatter_dimension=0, tiled=True)  150 us
    reduce_scatter x1, waiting for transfers between devices, per_device(): lax.psum_scatter(grad_query, ('dp', 'seq'), scatter_dimension=0, tiled=True)  91.1 us
    all_gather x1, blocking collectives, per_device(): lax.all_gather(b_up.astype(jnp.bfloat16), ('dp', 'seq'), axis=0, tiled=True)  82.8 us
    unnamed x2, blocking collectives  81.4 us
    all_to_all x1, waiting for transfers between devices, per_device(): lax.all_to_all(stacked, 'seq', split_axis=3, concat_axis=1, tiled=True)  80.5 us
  transfers between devices with their start and end apart: 16, of which 12 were waited for; matrix products, arithmetic and copies ran while one was open for 8% of the time, Pallas kernels for 0%

profile of v1, /device:TPU:0, one launch (start us, length us, event | category | flops | bytes accessed | tf_op | source)
XLA Modules:
  0.0 1859.5 jit_solution(4375514169695994829)
XLA Ops:
  7.3 1.7 convert_element_type.187
  9.1 1.5 convert_element_type.185
  10.8 1.5 convert_element_type.181
  12.4 1.5 convert_element_type.191
  14.0 1.8 convert_element_type.199
  18.8 42.5 %all-reduce.18 = (bf16[1024]{0:T(1024)(128)(2,1)S(1)}, bf16[1024]{0:T(1024)(128)(2,1)S(1)}, bf16[1024]{0:T(1024)(128)(2,1)S(1)}, bf16[1024]{0:T(1024)(128)(2,1)S...) all-reduce(bf16[1024]{0:T(1024)(128)(2,1)S(1)} %dynamic-update-slic, ...), channel_id=1, replica_groups=mesh['dp'=8,'seq'=4] {'dp','seq'}, use_global_device_ids=true, to_apply=%add.1 | all-reduce | flops 8192 | bytes 32768
  63.5 7.6 all-gather.12.cloned.1.call-done
  71.1 3.2 fusion.21
  75.5 54.4 %all-gather.10.cloned.1.call-done = bf16[1024,1024]{1,0:T(8,128)(2,1)} async-done(((bf16[32,1024]{1,0:T(8,128)(2,1)}), bf16[1024,1024]{1,0:T(8,128)(2,1)}) %all-gather.10.cloned.1.call-update) | async-done | bytes 2097168 | tf_op jit(solution)/shard_map/all_gather | solution.py:140
  129.9 2.4 convolution_convert_fusion.1
  132.5 56.2 %all-gather.8.cloned.1.call-done = bf16[1024,1024]{1,0:T(8,128)(2,1)} async-done(((bf16[32,1024]{1,0:T(8,128)(2,1)}), bf16[1024,1024]{1,0:T(8,128)(2,1)}) %all-gather.8.cloned.1.call-update) | async-done | bytes 2097168 | tf_op jit(solution)/shard_map/all_gather | solution.py:138
  188.7 2.6 fusion.20
  193.5 5.8 copy.102
  199.3 3.9 all-to-all-start
  203.2 80.5 %all-to-all-done = bf16[2,145,3,1024]{1,0,2,3:T(2,128)(2,1)S(1)} async-done(((bf16[2,145,3,1024]{1,0,2,3:T(2,128)(2,1)}), bf16[2,145,3,1024]{1,0,2,3:T(2,128)(2,1)S(1)}, u32[]{:S(2)}, u32[]{:S(2)}) %all-to-all-start) | async-done | bytes 1781792 | tf_op jit(solution)/shard_map/all_to_all | solution.py:179
  283.7 4.1 copy.146
  287.8 5.4 reshape.334
  293.2 9.7 while.22
  296.3 1.7 fusion.100
  298.3 1.4 fusion.98
  301.1 1.7 fusion.100
  304.2 3.5 all-to-all-start.1
  308.4 82.8 %all-gather = bf16[32,1,128]{2,1,0:T(2,128)(2,1)S(1)} all-gather(bf16[1,1,128]{2,1,0:T(2,128)(2,1)S(1)} %convert_bitcast_fusion), channel_id=1, replica_groups=mesh['dp'=8,'seq'=4] {'dp','seq'}, dimensions={0}, use_global_device_ids=true | all-gather | bytes 8448 | tf_op jit(solution)/shard_map/all_gather | solution.py:148
  392.9 3.0 fusion.36
  396.2 8.8 convolution_add_fusion
  405.0 42.7 %all-gather.18.cloned.1.call-done = bf16[4096,1024]{1,0:T(8,128)(2,1)} async-done(((bf16[128,1024]{1,0:T(8,128)(2,1)}), bf16[4096,1024]{1,0:T(8,128)(2,1)}) %all-gather.18.cloned.1.call-update) | async-done | bytes 8388624 | tf_op jit(solution)/shard_map/all_gather | solution.py:149
  447.7 8.7 fusion.19
  456.4 2.5 reshape.309
  458.9 3.7 fusion.32
  462.6 2.4 reshape.310
  465.0 9.0 convert_reduce_fusion
  474.0 6.4 multiply_reduce_fusion.1
  484.3 3.7 copy.110
  488.0 4.3 all-to-all-start.2
  492.3 4.4 fusion.29
  496.7 35.9 %all-to-all-done.2 = bf16[2,145,1024]{1,0,2:T(2,128)(2,1)} async-done(((bf16[2,145,1024]{1,0,2:T(2,128)(2,1)}), bf16[2,145,1024]{1,0,2:T(2,128)(2,1)}, u32[]{:S(2)}, u32[]{:S(2)}) %all-to-all-start.2) | async-done | bytes 593952 | tf_op jit(solution)/shard_map/all_to_all | solution.py:213
  532.6 3.0 copy.147
  535.6 2.4 reshape.333
  538.1 21.9 %while.23 = (s32[]{:T(128)}, bf16[2,580,3,256]{1,3,2,0:T(8,128)(2,1)}, bf16[2,580,3,256]{1,3,2,0:T(8,128)(2,1)S(1)}, s32[2,580]{1,0:T(2,128)S(1)}, f32[2,4,580]{...) while((s32[]{:T(128)}, bf16[2,580,3,256]{1,3,2,0:T(8,128)(2,1)}, ...), condition=%wide.region_12.13_spmd, body=%wide.region_10.12_spmd.sunk | while | flops 884781312 | bytes 63784960 | solution.py:214
  539.5 1.5 fusion.113
  541.0 2.0 multiply_reduce_fusion.10
  543.1 1.9 multiply_convert_fusion.6
  550.4 1.5 fusion.113
  552.0 2.0 multiply_reduce_fusion.10
  554.0 1.9 multiply_convert_fusion.6
  559.9 4.5 copy.115
  565.7 4.2 pad_maximum_fusion.1
  569.9 4.5 all-to-all-start.3
  576.0 62.2 %all-to-all-done.3 = bf16[4,2,145,3,256]{4,1,3,2,0:T(2,128)(2,1)} async-done(((bf16[4,2,145,3,256]{4,1,3,2,0:T(2,128)(2,1)}), bf16[4,2,145,3,256]{4,1,3,2,0:T(2,128)(2,1)}, u32[]{:S(2)}, u32[]{:S(2)}) %all-to-all-start.3) | async-done | bytes 1781792 | tf_op jit(solution)/shard_map/all_to_all | solution.py:216
  638.3 3.4 copy.119
  641.7 2.9 reshape_reshape.3
  644.5 3.3 fusion.23
  647.9 3.3 fusion.22
  651.3 3.4 fusion.25
  656.0 10.0 fusion.33
  667.3 10.7 fusion.26
  680.5 2.6 fusion.24
  687.0 1.4 copy.123
  688.7 38.9 %all-reduce.17 = (f32[1024]{0:T(1024)S(1)}, f32[1024]{0:T(1024)S(1)}, f32[1024]{0:T(1024)S(1)}, f32[1024]{0:T(1024)S(1)}, f32[1024]{0:T(1024)S(1)}, /*index=5*/f...) all-reduce(f32[1024]{0:T(1024)S(1)} %get-tuple-element.183, ...), channel_id=2, replica_groups=mesh['dp'=8,'seq'=4] {'dp','seq'}, use_global_device_ids=true, to_apply=%region_16.17.clone | all-reduce | flops 12288 | bytes 98304
  732.9 91.1 %reduce-scatter.7.cloned.1.call-done = f32[32,1024]{1,0:T(8,128)} async-done(((f32[1024,1024]{1,0:T(8,128)}), f32[32,1024]{1,0:T(8,128)}) %reduce-scatter.7.cloned.1.call-update) | async-done | bytes 131088 | tf_op jit(solution)/shard_map/reduce_scatter | solution.py:241
  823.9 150.4 %reduce-scatter.9.cloned.1.call-done = f32[32,1024]{1,0:T(8,128)} async-done(((f32[1024,1024]{1,0:T(8,128)}), f32[32,1024]{1,0:T(8,128)}) %reduce-scatter.9.cloned.1.call-update) | async-done | bytes 131088 | tf_op jit(solution)/shard_map/reduce_scatter | solution.py:243
  974.4 150.8 %reduce-scatter.11.cloned.1.call-done = f32[32,1024]{1,0:T(8,128)} async-done(((f32[1024,1024]{1,0:T(8,128)}), f32[32,1024]{1,0:T(8,128)}) %reduce-scatter.11.cloned.1.call-update) | async-done | bytes 131088 | tf_op jit(solution)/shard_map/reduce_scatter | solution.py:244
  1125.2 362.3 %reduce-scatter.15.cloned.1.call-done = f32[32,4096]{1,0:T(8,128)} async-done(((f32[1024,4096]{1,0:T(8,128)}), f32[32,4096]{1,0:T(8,128)}) %reduce-scatter.15.cloned.1.call-update) | async-done | bytes 524304 | tf_op jit(solution)/shard_map/reduce_scatter | solution.py:250
  1487.5 364.7 %reduce-scatter.17.cloned.1.call-done = f32[128,1024]{1,0:T(8,128)} async-done(((f32[4096,1024]{1,0:T(8,128)}), f32[128,1024]{1,0:T(8,128)}) %reduce-scatter.17.cloned.1.call-update) | async-done | bytes 524304 | tf_op jit(solution)/shard_map/reduce_scatter | solution.py:252
  (238 shorter events, 48.5 us)
Async XLA Ops:
  7.2 8.7 copy-start.22
  7.2 9.4 copy-start.35
  7.2 9.4 copy-start.36
  7.2 9.5 copy-start.37
  7.2 9.5 copy-start.38
  7.2 9.5 copy-start.39
  7.3 9.5 copy-start.40
  7.3 9.5 copy-start.41
  7.3 9.5 copy-start.42
  7.3 9.5 copy-start.7
  7.3 63.8 %all-gather.12.cloned.1.call-start = ((), (), s32[]{:S(2)}) async-start(), calls=%async_computation.12 | async-start | bytes 2162688 | tf_op jit(solution)/shard_map/all_gather | solution.py:141
  9.1 120.8 %all-gather.10.cloned.1.call-start = ((), (), s32[]{:S(2)}) async-start(), calls=%async_computation.11 | async-start | bytes 2162688 | tf_op jit(solution)/shard_map/all_gather | solution.py:140
  10.7 178.0 %all-gather.8.cloned.1.call-start = ((), (), s32[]{:S(2)}) async-start(), calls=%async_computation.10 | async-start | bytes 2162688 | tf_op jit(solution)/shard_map/all_gather | solution.py:138
  12.3 380.5 %all-gather.14.cloned.1.call-start = ((), (), s32[]{:S(2)}) async-start(), calls=%async_computation.13 | async-start | bytes 2162688 | tf_op jit(solution)/shard_map/all_gather | solution.py:143
  13.9 382.2 %all-gather.16.cloned.1.call-start = ((), (), s32[]{:S(2)}) async-start(), calls=%async_computation.14 | async-start | bytes 8650752 | tf_op jit(solution)/shard_map/all_gather | solution.py:147
  15.8 431.9 %all-gather.18.cloned.1.call-start = ((), (), s32[]{:S(2)}) async-start(), calls=%async_computation.15 | async-start | bytes 8650752 | tf_op jit(solution)/shard_map/all_gather | solution.py:149
  17.1 57.2 %copy-start.2 = (f32[290,1024]{1,0:T(8,128)}, f32[290,1024]{1,0:T(8,128)S(1)}, u32[]{:S(2)}) copy-start(f32[290,1024]{1,0:T(8,128)S(1)} %reshape.307) | copy-start | bytes 3563524
  61.3 9.8 copy-start.26
  61.3 9.8 copy-start.24
  61.9 9.2 copy-start.16
  62.9 11.4 copy-start.18
  63.1 11.2 copy-start.28
  63.2 11.1 copy-start.30
  63.5 66.4 %copy-start.21 = (bf16[290,1024]{1,0:T(8,128)(2,1)}, bf16[290,1024]{1,0:T(8,128)(2,1)S(1)}, u32[]{:S(2)}) copy-start(bf16[290,1024]{1,0:T(8,128)(2,1)S(1)} %add_convert_fusion.2) | copy-start | bytes 1781764
  199.3 84.4 %all-to-all-start = ((bf16[2,145,3,1024]{1,0,2,3:T(2,128)(2,1)}), bf16[2,145,3,1024]{1,0,2,3:T(2,128)(2,1)S(1)}, u32[]{:S(2)}, u32[]{:S(2)}) async-start(bf16[2,145,3,1024]{1,0,2,3:T(2,128)(2,1)} %copy.102), calls=%async_computation | async-start | bytes 6291456 | tf_op jit(solution)/shard_map/all_to_all | solution.py:179
  287.8 5.4 copy-start.20
  287.8 5.4 copy-start.23
  303.0 5.4 copy-start.43
  304.2 87.1 %all-to-all-start.1 = ((bf16[2,580,256]{2,0,1:T(2,128)(2,1)}), bf16[2,580,256]{2,0,1:T(2,128)(2,1)S(1)}, u32[]{:S(2)}, u32[]{:S(2)}) async-start(bf16[2,580,256]{2,0,1:T(2,128)(2,1)} %copy.106), calls=%async_computation.1 | async-start | bytes 1187840 | tf_op jit(solution)/shard_map/all_to_all | solution.py:181
  395.9 84.6 %copy-start = (f32[290,1024]{1,0:T(8,128)}, f32[290,1024]{1,0:T(8,128)S(1)}, u32[]{:S(2)}) copy-start(f32[290,1024]{1,0:T(8,128)S(1)} %get-tuple-element.250) | copy-start | bytes 3563524
  474.0 6.5 copy-start.12
  474.0 6.5 copy-start.9
  480.5 2.0 copy-start.34
  481.0 1.0 copy-start.4
  484.3 8.0 copy-start.5
  488.0 44.6 %all-to-all-start.2 = ((bf16[2,145,1024]{1,0,2:T(2,128)(2,1)}), bf16[2,145,1024]{1,0,2:T(2,128)(2,1)}, u32[]{:S(2)}, u32[]{:S(2)}) async-start(bf16[2,145,1024]{1,0,2:T(2,128)(2,1)} %copy.110), calls=%async_computation.2 | async-start | bytes 2097152 | tf_op jit(solution)/shard_map/all_to_all | solution.py:213
  492.3 240.6 %reduce-scatter.13.cloned.1.call-start = ((), (), s32[]{:S(2)}) async-start(), calls=%async_computation.19 | async-start | bytes 4325376 | tf_op jit(solution)/shard_map/reduce_scatter | solution.py:246
  546.0 1.6 copy-start.14
  547.7 1.3 copy-start.15
  556.9 1.6 copy-start.14
  558.6 1.3 copy-start.15
  569.9 4.8 copy-start.8
  569.9 4.8 copy-start.17
  569.9 4.8 copy-start.19
  569.9 4.8 copy-start.25
  569.9 4.9 copy-start.27
  569.9 68.4 %all-to-all-start.3 = ((bf16[4,2,145,3,256]{4,1,3,2,0:T(2,128)(2,1)}), bf16[4,2,145,3,256]{4,1,3,2,0:T(2,128)(2,1)}, u32[]{:S(2)}, u32[]{:S(2)}) async-start(bf16[4,2,145,3,256]{4,1,3,2,0:T(2,128)(2,1)} %pad_maximum_fusion.1), calls=%async_computation.3 | async-start | bytes 3563520 | tf_op jit(solution)/shard_map/all_to_all | solution.py:216
  574.5 249.4 %reduce-scatter.7.cloned.1.call-start = ((), (), s32[]{:S(2)}) async-start(), calls=%async_computation.16 | async-start | bytes 4325376 | tf_op jit(solution)/shard_map/reduce_scatter | solution.py:241
  647.9 326.5 %reduce-scatter.9.cloned.1.call-start = ((), (), s32[]{:S(2)}) async-start(), calls=%async_computation.17 | async-start | bytes 4325376 | tf_op jit(solution)/shard_map/reduce_scatter | solution.py:243
  651.2 474.0 %reduce-scatter.11.cloned.1.call-start = ((), (), s32[]{:S(2)}) async-start(), calls=%async_computation.18 | async-start | bytes 4325376 | tf_op jit(solution)/shard_map/reduce_scatter | solution.py:244
  654.7 1.3 copy-start.1
  654.7 832.8 %reduce-scatter.15.cloned.1.call-start = ((), (), s32[]{:S(2)}) async-start(), calls=%async_computation.20 | async-start | bytes 17301504 | tf_op jit(solution)/shard_map/reduce_scatter | solution.py:250
  666.0 1.3 copy-start.10
  666.0 1186.2 %reduce-scatter.17.cloned.1.call-start = ((), (), s32[]{:S(2)}) async-start(), calls=%async_computation.21 | async-start | bytes 17301504 | tf_op jit(solution)/shard_map/reduce_scatter | solution.py:252
  678.0 1.1 copy-start.11
  680.5 2.6 copy-start.13
  683.1 1.3 copy-start.3
  683.1 1.3 copy-start.29
  683.2 1.3 copy-start.31
  683.2 2.0 copy-start.33
  685.1 1.3 copy-start.6
  686.9 1.8 copy-start.32
Sparse Core Ops, SparseCore 0:
  11.6 59.4 all-gather.11
  74.6 55.2 all-gather.9
  133.4 55.1 all-gather.7
  192.0 93.7 all-gather.13
  289.2 79.5 all-gather.15
  372.1 75.5 all-gather.17
  496.8 175.8 reduce-scatter.12
  675.6 148.2 reduce-scatter.6
  826.8 147.5 reduce-scatter.8
  977.1 148.0 reduce-scatter.10
  1128.1 359.4 reduce-scatter.14
  1490.2 361.9 reduce-scatter.16
